TPU v7x, 32 devices: a whole 2x2x4 slice. The times are simulated.
32 devices in a mesh: cond: 4 (over y, core), seq: 8 (over z, x).
Axes of the slice: x: 2, y: 2, z: 4, core: 2. Of those that a mesh axis runs over, the one named last changes fastest.
Arguments:
- inputs: bfloat16 [4, 4096, 1024], P(None, 'seq', 'cond'), may hold values from -100 to 100
- coarse_ids: int32 [4, 1024], P(None, 'seq'), may hold values from 0 to 2047
- segment_ids: int32 [4, 4096], P(None, 'seq'), may hold values from 0 to 31, never falling along the last dimension, each value on 1 to 256 neighbouring positions
- cotangent: bfloat16 [4, 4096, 1024], P(None, 'seq', 'cond'), may hold values from -6 to 6
- embed_table: bfloat16 [2048, 1024], P('seq', 'cond'), may hold values from -6 to 6
- conv_weight: bfloat16 [3, 1024, 1024], P(None, 'cond', 'seq'), may hold values from -0.109375 to 0.109375
- res_weight: bfloat16 [1024, 1024], P('seq', 'cond'), may hold values from -0.1875 to 0.1875
- up_weight: bfloat16 [1024, 4096], P('cond', 'seq'), may hold values from -0.1875 to 0.1875
- gain_one: bfloat16 [1024], P(('cond', 'seq')), may hold values from 0.5 to 1.5
- shift_one: bfloat16 [1024], P(('cond', 'seq')), may hold values from -2 to 2
- qkv_weight: bfloat16 [1024, 3, 1024], P('seq', None, 'cond'), may hold values from -0.1875 to 0.1875
- out_weight: bfloat16 [1024, 1024], P('cond', 'seq'), may hold values from -0.5 to 0.5
- gain_two: bfloat16 [1024], P(('cond', 'seq')), may hold values from 0.5 to 1.5
- shift_two: bfloat16 [1024], P(('cond', 'seq')), may hold values from -2 to 2
- in_weight: bfloat16 [1024, 4096], P('seq', 'cond'), may hold values from -0.1875 to 0.1875
- down_weight: bfloat16 [4096, 1024], P('cond', 'seq'), may hold values from -0.09375 to 0.09375
Outputs:
- activation: bfloat16 [4, 4096, 1024], P(None, 'seq', 'cond')
- input_grad: bfloat16 [4, 4096, 1024], P(None, 'seq', 'cond')
- grad_table: float32 [2048, 1024], P('seq', 'cond')
- grad_conv: float32 [3, 1024, 1024], P(None, 'cond', 'seq')
- grad_res: float32 [1024, 1024], P('seq', 'cond')
- grad_up: float32 [1024, 4096], P('cond', 'seq')
- grad_gain_one: float32 [1024], P(('cond', 'seq'))
- grad_shift_one: float32 [1024], P(('cond', 'seq'))
- grad_qkv: float32 [1024, 3, 1024], P('seq', None, 'cond')
- grad_out: float32 [1024, 1024], P('cond', 'seq')
- grad_gain_two: float32 [1024], P(('cond', 'seq'))
- grad_shift_two: float32 [1024], P(('cond', 'seq'))
- grad_in: float32 [1024, 4096], P('seq', 'cond')
- grad_down: float32 [4096, 1024], P('cond', 'seq')
All inputs are finite; a program needn't handle non-finite values.
Results may differ from a plain program's by a relative error of at most 0.02.
Values may be sent and summed in bfloat16 or wider, within the bound.
No kernel may reach another device: no remote copies, remote signals or barrier semaphores. Data moves between devices by JAX's collectives and lax.ppermute only.
A program may use at most 112 MiB of HBM per device.

v0:
```python
import math
import jax
import jax.numpy as jnp
from jax import lax
from jax.sharding import PartitionSpec as P

HEAD = 64
ROW = 64
CONV_DILATION = 27
EPSILON = 1e-05
NEG_FILL = -1e30


def extended(cells, sides, width):
    for axis, dim in sides:
        count = lax.axis_size(axis)
        ends = count - 1
        head = lax.slice_in_dim(cells, 0, width, axis=dim)
        tail = lax.slice_in_dim(cells, cells.shape[dim] - width, cells.shape[dim], axis=dim)
        cells = jnp.concatenate(
            [
                lax.ppermute(tail, axis, [(i, (i + 1) % count) for i in range(ends)]),
                cells,
                lax.ppermute(head, axis, [((i + 1) % count, i) for i in range(ends)]),
            ],
            axis=dim,
        )
    return cells


def gelu_exact(value):
    return jax.nn.gelu(value, approximate=False)


def gelu_back(value, grad_value):
    _, pull = jax.vjp(gelu_exact, value)
    return pull(grad_value)[0]


def gram_dot(left, right):
    return lax.dot_general(
        left, right, (((0,), (0,)), ((), ())), preferred_element_type=jnp.float32
    )


def times_t(left, right):
    return lax.dot_general(
        left, right, (((1,), (1,)), ((), ())), preferred_element_type=jnp.float32
    )


def fetch_weights(shards):
    return (
        lax.all_gather(shards[0], "seq", axis=0, tiled=True),
        lax.all_gather(shards[1], "seq", axis=2, tiled=True),
        lax.all_gather(shards[2], "seq", axis=0, tiled=True),
        lax.all_gather(shards[3], "seq", axis=1, tiled=True),
        lax.all_gather(shards[4], "seq", axis=0, tiled=True),
        lax.all_gather(shards[5], "seq", axis=0, tiled=True),
        lax.all_gather(shards[6], "seq", axis=0, tiled=True),
        lax.all_gather(shards[7], "seq", axis=1, tiled=True),
        lax.all_gather(shards[8], "seq", axis=0, tiled=True),
        lax.all_gather(shards[9], "seq", axis=0, tiled=True),
        lax.all_gather(shards[10], "seq", axis=0, tiled=True),
        lax.all_gather(shards[11], "seq", axis=1, tiled=True),
    )


def spread_grads(gradients):
    return (
        lax.psum_scatter(
            gradients[0].astype(jnp.bfloat16), "seq", scatter_dimension=0, tiled=True
        ).astype(jnp.float32),
        lax.psum_scatter(
            gradients[1].astype(jnp.bfloat16), "seq", scatter_dimension=2, tiled=True
        ).astype(jnp.float32),
        lax.psum_scatter(
            gradients[2].astype(jnp.bfloat16), "seq", scatter_dimension=0, tiled=True
        ).astype(jnp.float32),
        lax.psum_scatter(
            gradients[3].astype(jnp.bfloat16), "seq", scatter_dimension=1, tiled=True
        ).astype(jnp.float32),
        lax.psum_scatter(
            gradients[4].astype(jnp.bfloat16), "seq", scatter_dimension=0, tiled=True
        ).astype(jnp.float32),
        lax.psum_scatter(
            gradients[5].astype(jnp.bfloat16), "seq", scatter_dimension=0, tiled=True
        ).astype(jnp.float32),
        lax.psum_scatter(
            gradients[6].astype(jnp.bfloat16), "seq", scatter_dimension=0, tiled=True
        ).astype(jnp.float32),
        lax.psum_scatter(
            gradients[7].astype(jnp.bfloat16), "seq", scatter_dimension=1, tiled=True
        ).astype(jnp.float32),
        lax.psum_scatter(
            gradients[8].astype(jnp.bfloat16), "seq", scatter_dimension=0, tiled=True
        ).astype(jnp.float32),
        lax.psum_scatter(
            gradients[9].astype(jnp.bfloat16), "seq", scatter_dimension=0, tiled=True
        ).astype(jnp.float32),
        lax.psum_scatter(
            gradients[10].astype(jnp.bfloat16), "seq", scatter_dimension=0, tiled=True
        ).astype(jnp.float32),
        lax.psum_scatter(
            gradients[11].astype(jnp.bfloat16), "seq", scatter_dimension=1, tiled=True
        ).astype(jnp.float32),
    )


def gather_rows(value):
    return lax.all_gather(value, "cond", axis=1, tiled=True)


def share_rows(value):
    return lax.psum_scatter(value, "cond", scatter_dimension=1, tiled=True)


def moments(first_part, second_part):
    return lax.psum((first_part, second_part), "cond")


def norm_forward(stream, full_width):
    tot_sum, tot_sq = moments(jnp.sum(stream, axis=1), jnp.sum(stream * stream, axis=1))
    mean_row = tot_sum / full_width
    var_row = tot_sq / full_width - mean_row * mean_row
    rstd_row = lax.rsqrt(var_row + EPSILON)
    return ((stream - mean_row[:, None]) * rstd_row[:, None], rstd_row)


def norm_backward(normed, rstd_row, gain, grad_norm, full_width):
    scaled = grad_norm * gain
    tot_first, tot_second = moments(jnp.sum(scaled, axis=1), jnp.sum(scaled * normed, axis=1))
    grad_stream = rstd_row[:, None] * (
        scaled - tot_first[:, None] / full_width - normed * tot_second[:, None] / full_width
    )
    return (grad_stream, jnp.sum(grad_norm * normed, axis=0), jnp.sum(grad_norm, axis=0))


def attend_scores(query_part, key_part, allowed, score_scale):
    scores = (
        jnp.einsum("bqhd,bkhd->bhqk", query_part, key_part, preferred_element_type=jnp.float32)
        * score_scale
    )
    return jnp.where(allowed, scores, NEG_FILL)


def one_micro(inputs, coarse, segments, cotangent, full):
    (
        embed_table,
        conv_weight,
        res_weight,
        up_weight,
        gain_one,
        shift_one,
        qkv_weight,
        out_weight,
        gain_two,
        shift_two,
        in_weight,
        down_weight,
    ) = full
    tokens, quarter = inputs.shape
    model_width = quarter * lax.axis_size("cond")
    coarse_length = coarse.shape[0]
    dilation_step = CONV_DILATION
    table_rows = embed_table.shape[0]
    onehot = (coarse[:, None] == jnp.arange(table_rows, dtype=jnp.int32)[None, :]).astype(
        jnp.bfloat16
    )
    embed = jnp.dot(onehot, embed_table, preferred_element_type=jnp.float32)
    coarse_activation_rows = gelu_exact(embed).astype(jnp.bfloat16)
    padded_input = extended(coarse_activation_rows, (("seq", 0),), dilation_step)
    kernel_tap_rows = jnp.concatenate(
        [
            padded_input[kernel_tap * dilation_step : kernel_tap * dilation_step + coarse_length]
            for kernel_tap in range(3)
        ],
        axis=1,
    )
    conv_flat = conv_weight.reshape(3 * quarter, model_width)
    conv_out = lax.psum(
        jnp.dot(kernel_tap_rows, conv_flat, preferred_element_type=jnp.float32), "cond"
    )
    mixed_act = gelu_exact(conv_out).astype(jnp.bfloat16)
    res_out = jnp.dot(mixed_act, res_weight, preferred_element_type=jnp.float32)
    hidden_cond = (embed + res_out).astype(jnp.bfloat16)
    up_terms = jnp.dot(hidden_cond, up_weight, preferred_element_type=jnp.float32).reshape(
        tokens, model_width
    )
    stream_zero = inputs.astype(jnp.float32) + share_rows(up_terms)
    gain_first = gain_one.astype(jnp.float32)
    gain_second = gain_two.astype(jnp.float32)
    normed_one, rstd_one = norm_forward(stream_zero, model_width)
    norm_one = gather_rows(
        (normed_one * gain_first + shift_one.astype(jnp.float32)).astype(jnp.bfloat16)
    )
    qkv_all = jnp.einsum(
        "td,dje->tje", norm_one, qkv_weight, preferred_element_type=jnp.float32
    ).astype(jnp.bfloat16)
    local_width = qkv_all.shape[2]
    head_count = local_width // HEAD
    row_count = tokens // ROW
    block_shape = (row_count, ROW, head_count, HEAD)
    query_part = qkv_all[:, 0].reshape(block_shape)
    key_part = qkv_all[:, 1].reshape(block_shape)
    value_part = qkv_all[:, 2].reshape(block_shape)
    seg_rows = segments.reshape(row_count, ROW)
    places = jnp.arange(ROW)
    allowed = (
        (seg_rows[:, :, None] == seg_rows[:, None, :]) & (places[:, None] >= places[None, :])[None]
    )[:, None]
    score_scale = 1.0 / math.sqrt(HEAD)
    scores = attend_scores(query_part, key_part, allowed, score_scale)
    row_max = jnp.max(scores, axis=-1, keepdims=True)
    row_exp = jnp.exp(scores - row_max)
    row_total = jnp.sum(row_exp, axis=-1, keepdims=True)
    log_total = row_max + jnp.log(row_total)
    probs_low = (row_exp / row_total).astype(jnp.bfloat16)
    context = jnp.einsum(
        "bhqk,bkhd->bqhd", probs_low, value_part, preferred_element_type=jnp.float32
    )
    context = context.astype(jnp.bfloat16).reshape(tokens, local_width)
    stream_one = stream_zero + share_rows(
        jnp.dot(context, out_weight, preferred_element_type=jnp.float32)
    )
    normed_two, rstd_two = norm_forward(stream_one, model_width)
    norm_two = gather_rows(
        (normed_two * gain_second + shift_two.astype(jnp.float32)).astype(jnp.bfloat16)
    )
    mlp_pre = jnp.dot(norm_two, in_weight, preferred_element_type=jnp.float32)
    mlp_act = gelu_exact(mlp_pre).astype(jnp.bfloat16)
    stream_two = stream_one + share_rows(
        jnp.dot(mlp_act, down_weight, preferred_element_type=jnp.float32)
    )
    result = stream_two.astype(jnp.bfloat16)
    cot_whole = gather_rows(cotangent)
    grad_down = gram_dot(mlp_act, cot_whole)
    grad_pre = gelu_back(mlp_pre, times_t(cot_whole, down_weight)).astype(jnp.bfloat16)
    grad_in = gram_dot(norm_two, grad_pre)
    grad_norm_two = share_rows(times_t(grad_pre, in_weight))
    back_two, grad_gain_two, grad_shift_two = norm_backward(
        normed_two, rstd_two, gain_second, grad_norm_two, model_width
    )
    grad_stream_one = cotangent.astype(jnp.float32) + back_two
    grad_att = gather_rows(grad_stream_one.astype(jnp.bfloat16))
    grad_out = gram_dot(context, grad_att)
    grad_context = times_t(grad_att, out_weight).astype(jnp.bfloat16).reshape(block_shape)
    attn_probs = jnp.exp(attend_scores(query_part, key_part, allowed, score_scale) - log_total)
    probs_low = attn_probs.astype(jnp.bfloat16)
    grad_probs = jnp.einsum(
        "bqhd,bkhd->bhqk", grad_context, value_part, preferred_element_type=jnp.float32
    )
    inner_row = jnp.sum(attn_probs * grad_probs, axis=-1, keepdims=True)
    grad_scores = (attn_probs * (grad_probs - inner_row)).astype(jnp.bfloat16)
    grad_query = (
        jnp.einsum("bhqk,bkhd->bqhd", grad_scores, key_part, preferred_element_type=jnp.float32)
        * score_scale
    ).astype(jnp.bfloat16)
    grad_keys = (
        jnp.einsum("bhqk,bqhd->bkhd", grad_scores, query_part, preferred_element_type=jnp.float32)
        * score_scale
    ).astype(jnp.bfloat16)
    grad_values = jnp.einsum(
        "bhqk,bqhd->bkhd", probs_low, grad_context, preferred_element_type=jnp.float32
    ).astype(jnp.bfloat16)
    grad_rows = jnp.stack(
        [
            grad_query.reshape(tokens, local_width),
            grad_keys.reshape(tokens, local_width),
            grad_values.reshape(tokens, local_width),
        ],
        axis=1,
    )
    grad_qkv = jnp.einsum("td,tje->dje", norm_one, grad_rows, preferred_element_type=jnp.float32)
    grad_norm_one = share_rows(
        jnp.einsum("tje,dje->td", grad_rows, qkv_weight, preferred_element_type=jnp.float32)
    )
    back_one, grad_gain_one, grad_shift_one = norm_backward(
        normed_one, rstd_one, gain_first, grad_norm_one, model_width
    )
    input_grad = (grad_stream_one + back_one).astype(jnp.bfloat16)
    grad_up_rows = gather_rows(input_grad).reshape(coarse_length, 4 * model_width)
    grad_up = gram_dot(hidden_cond, grad_up_rows)
    grad_hidden = times_t(grad_up_rows, up_weight)
    grad_res_low = grad_hidden.astype(jnp.bfloat16)
    grad_res = gram_dot(mixed_act, grad_res_low)
    grad_mixed = lax.psum(times_t(grad_res_low, res_weight).astype(jnp.bfloat16), "cond").astype(
        jnp.float32
    )
    grad_conv_low = gelu_back(conv_out, grad_mixed).astype(jnp.bfloat16)
    grad_conv = gram_dot(kernel_tap_rows, grad_conv_low).reshape(3, quarter, model_width)
    grad_taps = times_t(grad_conv_low, conv_flat)
    grad_padded = jnp.pad(grad_taps[:, 0:quarter], ((0, 2 * dilation_step), (0, 0)))
    grad_padded = grad_padded + jnp.pad(
        grad_taps[:, quarter : 2 * quarter], ((dilation_step, dilation_step), (0, 0))
    )
    grad_padded = grad_padded + jnp.pad(
        grad_taps[:, 2 * quarter :], ((2 * dilation_step, 0), (0, 0))
    )
    rim_grads = jnp.concatenate(
        [grad_padded[:dilation_step], grad_padded[coarse_length + dilation_step :]], axis=0
    )
    rim_values = extended(rim_grads.astype(jnp.bfloat16), (("seq", 0),), dilation_step).astype(
        rim_grads.dtype
    )
    grad_act = grad_padded[dilation_step : dilation_step + coarse_length]
    grad_act = grad_act + jnp.pad(
        rim_values[:dilation_step], ((0, coarse_length - dilation_step), (0, 0))
    )
    grad_act = grad_act + jnp.pad(
        rim_values[3 * dilation_step :], ((coarse_length - dilation_step, 0), (0, 0))
    )
    grad_embed = (grad_hidden + gelu_back(embed, grad_act)).astype(jnp.bfloat16)
    grad_table = gram_dot(onehot, grad_embed)
    gradients = (
        grad_table,
        grad_conv,
        grad_res,
        grad_up,
        grad_gain_one,
        grad_shift_one,
        grad_qkv,
        grad_out,
        grad_gain_two,
        grad_shift_two,
        grad_in,
        grad_down,
    )
    return (result, input_grad, gradients)


def on_device(
    inputs,
    coarse_ids,
    segment_ids,
    cotangent,
    embed_table,
    conv_weight,
    res_weight,
    up_weight,
    gain_one,
    shift_one,
    qkv_weight,
    out_weight,
    gain_two,
    shift_two,
    in_weight,
    down_weight,
):
    shards = (
        embed_table,
        conv_weight,
        res_weight,
        up_weight,
        gain_one,
        shift_one,
        qkv_weight,
        out_weight,
        gain_two,
        shift_two,
        in_weight,
        down_weight,
    )
    outputs = []
    in_grads = []
    summed = None
    for index in range(inputs.shape[0]):
        full = fetch_weights(shards)
        result, input_grad, gradients = one_micro(
            inputs[index], coarse_ids[index], segment_ids[index], cotangent[index], full
        )
        outputs.append(result)
        in_grads.append(input_grad)
        shares = spread_grads(gradients)
        summed = shares if summed is None else jax.tree.map(jnp.add, summed, shares)
    return (jnp.stack(outputs), jnp.stack(in_grads)) + tuple(summed)


def solution(mesh):
    return jax.shard_map(
        on_device,
        mesh=mesh,
        in_specs=(
            P(None, "seq", "cond"),
            P(None, "seq"),
            P(None, "seq"),
            P(None, "seq", "cond"),
            P("seq", "cond"),
            P(None, "cond", "seq"),
            P("seq", "cond"),
            P("cond", "seq"),
            P(("cond", "seq")),
            P(("cond", "seq")),
            P("seq", None, "cond"),
            P("cond", "seq"),
            P(("cond", "seq")),
            P(("cond", "seq")),
            P("seq", "cond"),
            P("cond", "seq"),
        ),
        out_specs=(
            P(None, "seq", "cond"),
            P(None, "seq", "cond"),
            P("seq", "cond"),
            P(None, "cond", "seq"),
            P("seq", "cond"),
            P("cond", "seq"),
            P(("cond", "seq")),
            P(("cond", "seq")),
            P("seq", None, "cond"),
            P("cond", "seq"),
            P(("cond", "seq")),
            P(("cond", "seq")),
            P("seq", "cond"),
            P("cond", "seq"),
        ),
        check_vma=False,
    )
```

profile of v0, /device:TPU:0, one launch (start us, length us, event | category | flops | bytes accessed | tf_op | source)
XLA Modules:
  0.0 3656.3 jit_solution(12000477826808269472)
XLA Ops:
  9.6 43.4 %all-gather.31.cloned.1.call-done = bf16[2048,256]{1,0:T(8,128)(2,1)} async-done(((bf16[256,256]{1,0:T(8,128)(2,1)}), bf16[2048,256]{1,0:T(8,128)(2,1)}) %all-gather.31.cloned.1.call-update) | async-done | bytes 1048592 | tf_op jit(solution)/shard_map/all_gather | solution.py:54
  77.3 22.3 all-gather.33.cloned.1.call-done
  111.0 31.5 all_gather.66
  142.5 19.0 all-reduce.51.cloned.1.call-done
  166.6 48.3 %all-gather.35.cloned.1.call-done = bf16[256,4096]{1,0:T(8,128)(2,1)} async-done(((bf16[256,512]{1,0:T(8,128)(2,1)}), bf16[256,4096]{1,0:T(8,128)(2,1)}) %all-gather.35.cloned.1.call-update) | async-done | bytes 2097168 | tf_op jit(solution)/shard_map/all_gather | solution.py:57
  246.0 18.9 all-reduce.46
  265.0 17.2 reduce-scatter.83.cloned.1.call-done
  282.2 34.2 reduce-scatter.89.cloned.1.call-done
  316.4 34.0 reduce-scatter.95.cloned.1.call-done
  366.3 29.8 all_gather.140
  402.3 17.5 all-gather.55.cloned.1.call-done
  491.8 19.1 reduce-scatter.97.cloned.1.call-done
  512.8 31.9 reduce-scatter.91.cloned.1.call-done
  546.0 32.8 reduce-scatter.85.cloned.1.call-done
  580.0 32.6 reduce-scatter.79.cloned.1.call-done
  633.8 30.3 all-gather.43.cloned.1.call-done
  664.1 17.6 all-gather.57.cloned.1.call-done
  700.0 53.4 %all-gather.45.cloned.1.call-done = bf16[1024,1024]{1,0:T(8,128)(2,1)} async-done(((bf16[1024,128]{1,0:T(8,128)(2,1)}), bf16[1024,1024]{1,0:T(8,128)(2,1)}) %all-gather.45.cloned.1.call-update) | async-done | bytes 2097168 | tf_op jit(solution)/shard_map/all_gather | solution.py:65
  898.1 34.0 reduce-scatter.109.cloned.1.call-done
  932.1 34.0 reduce-scatter.105.cloned.1.call-done
  966.1 34.0 reduce-scatter.101.cloned.1.call-done
  1013.4 20.9 reduce-scatter.99.cloned.1.call-done
  1034.3 33.8 reduce-scatter.81.cloned.1.call-done
  1071.9 30.4 reduce-scatter.93.cloned.1.call-done
  1102.3 34.0 reduce-scatter.87.cloned.1.call-done
  1140.2 15.0 all-gather.65.cloned.1.call-done
  1222.2 23.0 reduce-scatter.115.cloned.1.call-done
  1245.2 34.0 reduce-scatter.103.cloned.1.call-done
  1279.2 34.2 reduce-scatter.111.cloned.1.call-done
  1313.4 33.8 reduce-scatter.107.cloned.1.call-done
  1384.0 15.9 all-gather.71.cloned.1.call-done
  1402.4 16.4 all-gather.67.cloned.1.call-done
  1601.5 19.8 reduce-scatter.177.cloned.1.call-done
  1622.4 69.0 %reduce-scatter.175.cloned.1.call-done = bf16[128,1024]{1,0:T(8,128)(2,1)} async-done(((bf16[1024,1024]{1,0:T(8,128)(2,1)}), bf16[128,1024]{1,0:T(8,128)(2,1)}) %reduce-scatter.175.cloned.1.call-update) | async-done | bytes 262160
  1692.5 69.1 %reduce-scatter.173.cloned.1.call-done = bf16[128,1024]{1,0:T(8,128)(2,1)} async-done(((bf16[1024,1024]{1,0:T(8,128)(2,1)}), bf16[128,1024]{1,0:T(8,128)(2,1)}) %reduce-scatter.173.cloned.1.call-update) | async-done | bytes 262160
  1764.9 66.7 %reduce-scatter.155.cloned.1.call-done = bf16[128,1024]{1,0:T(8,128)(2,1)} async-done(((bf16[1024,1024]{1,0:T(8,128)(2,1)}), bf16[128,1024]{1,0:T(8,128)(2,1)}) %reduce-scatter.155.cloned.1.call-update) | async-done | bytes 262160 | tf_op jit(solution)/shard_map/reduce_scatter | solution.py:101
  1831.7 70.3 %reduce-scatter.153.cloned.1.call-done = bf16[128,1024]{1,0:T(8,128)(2,1)} async-done(((bf16[1024,1024]{1,0:T(8,128)(2,1)}), bf16[128,1024]{1,0:T(8,128)(2,1)}) %reduce-scatter.153.cloned.1.call-update) | async-done | bytes 262160 | tf_op jit(solution)/shard_map/reduce_scatter | solution.py:101
  1902.0 70.2 %reduce-scatter.151.cloned.1.call-done = bf16[128,1024]{1,0:T(8,128)(2,1)} async-done(((bf16[1024,1024]{1,0:T(8,128)(2,1)}), bf16[128,1024]{1,0:T(8,128)(2,1)}) %reduce-scatter.151.cloned.1.call-update) | async-done | bytes 262160 | tf_op jit(solution)/shard_map/reduce_scatter | solution.py:101
  1972.2 70.2 %reduce-scatter.149.cloned.1.call-done = bf16[128,1024]{1,0:T(8,128)(2,1)} async-done(((bf16[1024,1024]{1,0:T(8,128)(2,1)}), bf16[128,1024]{1,0:T(8,128)(2,1)}) %reduce-scatter.149.cloned.1.call-update) | async-done | bytes 262160 | tf_op jit(solution)/shard_map/reduce_scatter | solution.py:101
  2044.6 62.7 %reduce-scatter.171.cloned.1.call-done = bf16[128,256]{1,0:T(8,128)(2,1)} async-done(((bf16[1024,256]{1,0:T(8,128)(2,1)}), bf16[128,256]{1,0:T(8,128)(2,1)}) %reduce-scatter.171.cloned.1.call-update) | async-done | bytes 65552
  2108.2 63.6 %reduce-scatter.165.cloned.1.call-done = bf16[128,256]{1,0:T(8,128)(2,1)} async-done(((bf16[1024,256]{1,0:T(8,128)(2,1)}), bf16[128,256]{1,0:T(8,128)(2,1)}) %reduce-scatter.165.cloned.1.call-update) | async-done | bytes 65552
  2172.8 63.1 %reduce-scatter.169.cloned.1.call-done = bf16[128,256]{1,0:T(8,128)(2,1)} async-done(((bf16[1024,256]{1,0:T(8,128)(2,1)}), bf16[128,256]{1,0:T(8,128)(2,1)}) %reduce-scatter.169.cloned.1.call-update) | async-done | bytes 65552
  2236.8 63.8 %reduce-scatter.167.cloned.1.call-done = bf16[128,256]{1,0:T(8,128)(2,1)} async-done(((bf16[1024,256]{1,0:T(8,128)(2,1)}), bf16[128,256]{1,0:T(8,128)(2,1)}) %reduce-scatter.167.cloned.1.call-update) | async-done | bytes 65552
  2302.3 66.3 %reduce-scatter.145.cloned.1.call-done = bf16[128,3,256]{2,0,1:T(8,128)(2,1)} async-done(((bf16[1024,3,256]{2,0,1:T(8,128)(2,1)}), bf16[128,3,256]{2,0,1:T(8,128)(2,1)}) %reduce-scatter.145.cloned.1.call-update) | async-done | bytes 196624 | tf_op jit(solution)/shard_map/reduce_scatter | solution.py:89
  2368.6 68.4 %reduce-scatter.143.cloned.1.call-done = bf16[128,3,256]{2,0,1:T(8,128)(2,1)} async-done(((bf16[1024,3,256]{2,0,1:T(8,128)(2,1)}), bf16[128,3,256]{2,0,1:T(8,128)(2,1)}) %reduce-scatter.143.cloned.1.call-update) | async-done | bytes 196624 | tf_op jit(solution)/shard_map/reduce_scatter | solution.py:89
  2437.0 67.8 %reduce-scatter.141.cloned.1.call-done = bf16[128,3,256]{2,0,1:T(8,128)(2,1)} async-done(((bf16[1024,3,256]{2,0,1:T(8,128)(2,1)}), bf16[128,3,256]{2,0,1:T(8,128)(2,1)}) %reduce-scatter.141.cloned.1.call-update) | async-done | bytes 196624 | tf_op jit(solution)/shard_map/reduce_scatter | solution.py:89
  2504.8 68.2 %reduce-scatter.147.cloned.1.call-done = bf16[128,3,256]{2,0,1:T(8,128)(2,1)} async-done(((bf16[1024,3,256]{2,0,1:T(8,128)(2,1)}), bf16[128,3,256]{2,0,1:T(8,128)(2,1)}) %reduce-scatter.147.cloned.1.call-update) | async-done | bytes 196624 | tf_op jit(solution)/shard_map/reduce_scatter | solution.py:89
  2575.2 19.8 all-reduce.45
  2598.5 38.8 %reduce-scatter.127.cloned.1.call-done = bf16[128,256]{1,0:T(8,128)(2,1)} async-done(((bf16[1024,256]{1,0:T(8,128)(2,1)}), bf16[128,256]{1,0:T(8,128)(2,1)}) %reduce-scatter.127.cloned.1.call-update) | async-done | bytes 65552 | tf_op jit(solution)/shard_map/reduce_scatter | solution.py:77
  2637.3 64.5 %reduce-scatter.129.cloned.1.call-done = bf16[128,256]{1,0:T(8,128)(2,1)} async-done(((bf16[1024,256]{1,0:T(8,128)(2,1)}), bf16[128,256]{1,0:T(8,128)(2,1)}) %reduce-scatter.129.cloned.1.call-update) | async-done | bytes 65552 | tf_op jit(solution)/shard_map/reduce_scatter | solution.py:77
  2701.8 64.2 %reduce-scatter.125.cloned.1.call-done = bf16[128,256]{1,0:T(8,128)(2,1)} async-done(((bf16[1024,256]{1,0:T(8,128)(2,1)}), bf16[128,256]{1,0:T(8,128)(2,1)}) %reduce-scatter.125.cloned.1.call-update) | async-done | bytes 65552 | tf_op jit(solution)/shard_map/reduce_scatter | solution.py:77
  2765.9 64.7 %reduce-scatter.131.cloned.1.call-done = bf16[128,256]{1,0:T(8,128)(2,1)} async-done(((bf16[1024,256]{1,0:T(8,128)(2,1)}), bf16[128,256]{1,0:T(8,128)(2,1)}) %reduce-scatter.131.cloned.1.call-update) | async-done | bytes 65552 | tf_op jit(solution)/shard_map/reduce_scatter | solution.py:77
  2832.3 64.2 %reduce-scatter.117.cloned.1.call-done = bf16[256,256]{1,0:T(8,128)(2,1)} async-done(((bf16[2048,256]{1,0:T(8,128)(2,1)}), bf16[256,256]{1,0:T(8,128)(2,1)}) %reduce-scatter.117.cloned.1.call-update) | async-done | bytes 131088 | tf_op jit(solution)/shard_map/reduce_scatter | solution.py:71
  2896.5 66.2 %reduce-scatter.119.cloned.1.call-done = bf16[256,256]{1,0:T(8,128)(2,1)} async-done(((bf16[2048,256]{1,0:T(8,128)(2,1)}), bf16[256,256]{1,0:T(8,128)(2,1)}) %reduce-scatter.119.cloned.1.call-update) | async-done | bytes 131088 | tf_op jit(solution)/shard_map/reduce_scatter | solution.py:71
  2962.6 65.8 %reduce-scatter.121.cloned.1.call-done = bf16[256,256]{1,0:T(8,128)(2,1)} async-done(((bf16[2048,256]{1,0:T(8,128)(2,1)}), bf16[256,256]{1,0:T(8,128)(2,1)}) %reduce-scatter.121.cloned.1.call-update) | async-done | bytes 131088 | tf_op jit(solution)/shard_map/reduce_scatter | solution.py:71
  3028.4 66.0 %reduce-scatter.123.cloned.1.call-done = bf16[256,256]{1,0:T(8,128)(2,1)} async-done(((bf16[2048,256]{1,0:T(8,128)(2,1)}), bf16[256,256]{1,0:T(8,128)(2,1)}) %reduce-scatter.123.cloned.1.call-update) | async-done | bytes 131088 | tf_op jit(solution)/shard_map/reduce_scatter | solution.py:71
  3096.3 65.2 %reduce-scatter.157.cloned.1.call-done = bf16[128,768]{1,0:T(8,128)(2,1)} async-done(((bf16[1024,768]{1,0:T(8,128)(2,1)}), bf16[128,768]{1,0:T(8,128)(2,1)}) %reduce-scatter.157.cloned.1.call-update) | async-done | bytes 196624
  3162.7 66.2 %reduce-scatter.159.cloned.1.call-done = bf16[128,768]{1,0:T(8,128)(2,1)} async-done(((bf16[1024,768]{1,0:T(8,128)(2,1)}), bf16[128,768]{1,0:T(8,128)(2,1)}) %reduce-scatter.159.cloned.1.call-update) | async-done | bytes 196624
  3230.2 65.9 %reduce-scatter.161.cloned.1.call-done = bf16[128,768]{1,0:T(8,128)(2,1)} async-done(((bf16[1024,768]{1,0:T(8,128)(2,1)}), bf16[128,768]{1,0:T(8,128)(2,1)}) %reduce-scatter.161.cloned.1.call-update) | async-done | bytes 196624
  3297.3 66.3 %reduce-scatter.163.cloned.1.call-done = bf16[128,768]{1,0:T(8,128)(2,1)} async-done(((bf16[1024,768]{1,0:T(8,128)(2,1)}), bf16[128,768]{1,0:T(8,128)(2,1)}) %reduce-scatter.163.cloned.1.call-update) | async-done | bytes 196624
  3365.7 68.7 %reduce-scatter.135.cloned.1.call-done = bf16[256,512]{1,0:T(8,128)(2,1)} async-done(((bf16[256,4096]{1,0:T(8,128)(2,1)}), bf16[256,512]{1,0:T(8,128)(2,1)}) %reduce-scatter.135.cloned.1.call-update) | async-done | bytes 262160 | tf_op jit(solution)/shard_map/reduce_scatter | solution.py:80
  3434.4 70.8 %reduce-scatter.137.cloned.1.call-done = bf16[256,512]{1,0:T(8,128)(2,1)} async-done(((bf16[256,4096]{1,0:T(8,128)(2,1)}), bf16[256,512]{1,0:T(8,128)(2,1)}) %reduce-scatter.137.cloned.1.call-update) | async-done | bytes 262160 | tf_op jit(solution)/shard_map/reduce_scatter | solution.py:80
  3505.2 71.0 %reduce-scatter.133.cloned.1.call-done = bf16[256,512]{1,0:T(8,128)(2,1)} async-done(((bf16[256,4096]{1,0:T(8,128)(2,1)}), bf16[256,512]{1,0:T(8,128)(2,1)}) %reduce-scatter.133.cloned.1.call-update) | async-done | bytes 262160 | tf_op jit(solution)/shard_map/reduce_scatter | solution.py:80
  3576.2 70.8 %reduce-scatter.139.cloned.1.call-done = bf16[256,512]{1,0:T(8,128)(2,1)} async-done(((bf16[256,4096]{1,0:T(8,128)(2,1)}), bf16[256,512]{1,0:T(8,128)(2,1)}) %reduce-scatter.139.cloned.1.call-update) | async-done | bytes 262160 | tf_op jit(solution)/shard_map/reduce_scatter | solution.py:80
  (987 shorter events, 690.2 us)
Async XLA Ops:
  8.7 152.9 %all-reduce.51.cloned.1.call-start = ((), (), s32[]{:S(2)}) async-start(), calls=%async_computation.130 | async-start | bytes 4194304 | tf_op jit(solution)/shard_map/psum | solution.py:181
  111.0 154.0 %reduce-scatter.77.cloned.1.call-start = ((), (), s32[]{:S(2)}) async-start(), calls=%async_computation.55 | async-start | bytes 2621440 | tf_op jit(solution)/shard_map/reduce_scatter | solution.py:115
  237.2 113.1 %reduce-scatter.95.cloned.1.call-start = ((), (), s32[]{:S(2)}) async-start(), calls=%async_computation.73 | async-start | bytes 2621440 | tf_op jit(solution)/shard_map/reduce_scatter | solution.py:115
  242.9 159.4 %all-gather.39.cloned.1.call-start = ((), (), s32[]{:S(2)}) async-start(), calls=%async_computation.57 | async-start | bytes 1769472 | tf_op jit(solution)/shard_map/all_gather | solution.py:60
  243.7 176.1 %all-gather.55.cloned.1.call-start = ((), (), s32[]{:S(2)}) async-start(), calls=%async_computation.74 | async-start | bytes 1310720 | tf_op jit(solution)/shard_map/all_gather | solution.py:111
  365.9 111.0 %all-gather.37.cloned.1.call-start = ((), (), s32[]{:S(2)}) async-start(), calls=%async_computation.56 | async-start | bytes 1310720 | tf_op jit(solution)/shard_map/all_gather | solution.py:111
  397.2 113.7 %reduce-scatter.97.cloned.1.call-start = ((), (), s32[]{:S(2)}) async-start(), calls=%async_computation.75 | async-start | bytes 2621440 | tf_op jit(solution)/shard_map/reduce_scatter | solution.py:115
  455.1 123.7 %reduce-scatter.85.cloned.1.call-start = ((), (), s32[]{:S(2)}) async-start(), calls=%async_computation.65 | async-start | bytes 2621440 | tf_op jit(solution)/shard_map/reduce_scatter | solution.py:115
  474.1 138.5 %reduce-scatter.79.cloned.1.call-start = ((), (), s32[]{:S(2)}) async-start(), calls=%async_computation.58 | async-start | bytes 2621440 | tf_op jit(solution)/shard_map/reduce_scatter | solution.py:115
  491.2 172.9 %all-gather.43.cloned.1.call-start = ((), (), s32[]{:S(2)}) async-start(), calls=%async_computation.60 | async-start | bytes 2359296 | tf_op jit(solution)/shard_map/all_gather | solution.py:64
  491.8 189.9 %all-gather.57.cloned.1.call-start = ((), (), s32[]{:S(2)}) async-start(), calls=%async_computation.76 | async-start | bytes 1310720 | tf_op jit(solution)/shard_map/all_gather | solution.py:111
  628.9 124.5 %all-gather.45.cloned.1.call-start = ((), (), s32[]{:S(2)}) async-start(), calls=%async_computation.61 | async-start | bytes 2359296 | tf_op jit(solution)/shard_map/all_gather | solution.py:65
  629.6 141.0 %all-gather.53.cloned.1.call-start = ((), (), s32[]{:S(2)}) async-start(), calls=%async_computation.71 | async-start | bytes 1310720 | tf_op jit(solution)/shard_map/all_gather | solution.py:111
  630.4 158.8 %all-gather.79.cloned.1.call-start = ((), (), s32[]{:S(2)}) async-start(), calls=%async_computation.116 | async-start | bytes 1310720 | tf_op jit(solution)/shard_map/all_gather | solution.py:111
  631.1 177.0 %all-gather.49.cloned.1.call-start = ((), (), s32[]{:S(2)}) async-start(), calls=%async_computation.66 | async-start | bytes 1310720 | tf_op jit(solution)/shard_map/all_gather | solution.py:111
  631.7 194.9 %all-gather.77.cloned.1.call-start = ((), (), s32[]{:S(2)}) async-start(), calls=%async_computation.115 | async-start | bytes 1310720 | tf_op jit(solution)/shard_map/all_gather | solution.py:111
  632.4 213.1 %all-gather.41.cloned.1.call-start = ((), (), s32[]{:S(2)}) async-start(), calls=%async_computation.59 | async-start | bytes 1310720 | tf_op jit(solution)/shard_map/all_gather | solution.py:111
  633.0 230.9 %all-gather.75.cloned.1.call-start = ((), (), s32[]{:S(2)}) async-start(), calls=%async_computation.114 | async-start | bytes 1310720 | tf_op jit(solution)/shard_map/all_gather | solution.py:111
  633.6 264.5 %reduce-scatter.113.cloned.1.call-start = ((), (), s32[]{:S(2)}) async-start(), calls=%async_computation.87 | async-start | bytes 2621440 | tf_op jit(solution)/shard_map/reduce_scatter | solution.py:115
  762.1 170.0 %reduce-scatter.109.cloned.1.call-start = ((), (), s32[]{:S(2)}) async-start(), calls=%async_computation.84 | async-start | bytes 2621440 | tf_op jit(solution)/shard_map/reduce_scatter | solution.py:115
  798.0 168.1 %reduce-scatter.105.cloned.1.call-start = ((), (), s32[]{:S(2)}) async-start(), calls=%async_computation.81 | async-start | bytes 2621440 | tf_op jit(solution)/shard_map/reduce_scatter | solution.py:115
  835.4 164.7 %reduce-scatter.101.cloned.1.call-start = ((), (), s32[]{:S(2)}) async-start(), calls=%async_computation.78 | async-start | bytes 2621440 | tf_op jit(solution)/shard_map/reduce_scatter | solution.py:115
  872.6 161.7 %reduce-scatter.99.cloned.1.call-start = ((), (), s32[]{:S(2)}) async-start(), calls=%async_computation.77 | async-start | bytes 2621440 | tf_op jit(solution)/shard_map/reduce_scatter | solution.py:115
  877.5 190.6 %reduce-scatter.81.cloned.1.call-start = ((), (), s32[]{:S(2)}) async-start(), calls=%async_computation.62 | async-start | bytes 2621440 | tf_op jit(solution)/shard_map/reduce_scatter | solution.py:115
  882.5 219.8 %reduce-scatter.93.cloned.1.call-start = ((), (), s32[]{:S(2)}) async-start(), calls=%async_computation.72 | async-start | bytes 2621440 | tf_op jit(solution)/shard_map/reduce_scatter | solution.py:115
  887.5 248.8 %reduce-scatter.87.cloned.1.call-start = ((), (), s32[]{:S(2)}) async-start(), calls=%async_computation.67 | async-start | bytes 2621440 | tf_op jit(solution)/shard_map/reduce_scatter | solution.py:115
  892.0 263.2 %all-gather.65.cloned.1.call-start = ((), (), s32[]{:S(2)}) async-start(), calls=%async_computation.88 | async-start | bytes 1310720 | tf_op jit(solution)/shard_map/all_gather | solution.py:111
  1071.8 120.8 %all-gather.63.cloned.1.call-start = ((), (), s32[]{:S(2)}) async-start(), calls=%async_computation.85 | async-start | bytes 1310720 | tf_op jit(solution)/shard_map/all_gather | solution.py:111
  1191.4 121.9 %reduce-scatter.111.cloned.1.call-start = ((), (), s32[]{:S(2)}) async-start(), calls=%async_computation.86 | async-start | bytes 2621440 | tf_op jit(solution)/shard_map/reduce_scatter | solution.py:115
  1206.4 140.8 %reduce-scatter.107.cloned.1.call-start = ((), (), s32[]{:S(2)}) async-start(), calls=%async_computation.83 | async-start | bytes 2621440 | tf_op jit(solution)/shard_map/reduce_scatter | solution.py:115
  1222.2 159.4 %all-gather.69.cloned.1.call-start = ((), (), s32[]{:S(2)}) async-start(), calls=%async_computation.92 | async-start | bytes 1310720 | tf_op jit(solution)/shard_map/all_gather | solution.py:111
  1367.3 143.5 %all-reduce.53.cloned.1.call-start = ((), (), s32[]{:S(2)}) async-start(), calls=%async_computation.131 | async-start | bytes 2097152 | tf_op jit(solution)/shard_map/psum | solution.py:287
  1442.8 157.6 %reduce-scatter.179.cloned.1.call-start = ((), (), s32[]{:S(2)}) async-start(), calls=%async_computation.129 | async-start | bytes 2359296
  1448.2 173.0 %reduce-scatter.177.cloned.1.call-start = ((), (), s32[]{:S(2)}) async-start(), calls=%async_computation.128 | async-start | bytes 2359296
  1454.6 236.8 %reduce-scatter.175.cloned.1.call-start = ((), (), s32[]{:S(2)}) async-start(), calls=%async_computation.127 | async-start | bytes 2359296
  1460.9 300.7 %reduce-scatter.173.cloned.1.call-start = ((), (), s32[]{:S(2)}) async-start(), calls=%async_computation.126 | async-start | bytes 2359296
  1467.2 364.4 %reduce-scatter.155.cloned.1.call-start = ((), (), s32[]{:S(2)}) async-start(), calls=%async_computation.113 | async-start | bytes 2359296 | tf_op jit(solution)/shard_map/reduce_scatter | solution.py:101
  1471.5 430.4 %reduce-scatter.153.cloned.1.call-start = ((), (), s32[]{:S(2)}) async-start(), calls=%async_computation.112 | async-start | bytes 2359296 | tf_op jit(solution)/shard_map/reduce_scatter | solution.py:101
  1475.7 496.5 %reduce-scatter.151.cloned.1.call-start = ((), (), s32[]{:S(2)}) async-start(), calls=%async_computation.111 | async-start | bytes 2359296 | tf_op jit(solution)/shard_map/reduce_scatter | solution.py:101
  1479.8 562.6 %reduce-scatter.149.cloned.1.call-start = ((), (), s32[]{:S(2)}) async-start(), calls=%async_computation.110 | async-start | bytes 2359296 | tf_op jit(solution)/shard_map/reduce_scatter | solution.py:101
  1484.0 623.3 %reduce-scatter.171.cloned.1.call-start = ((), (), s32[]{:S(2)}) async-start(), calls=%async_computation.125 | async-start | bytes 589824
  1486.8 685.0 %reduce-scatter.165.cloned.1.call-start = ((), (), s32[]{:S(2)}) async-start(), calls=%async_computation.122 | async-start | bytes 589824
  1488.3 747.6 %reduce-scatter.169.cloned.1.call-start = ((), (), s32[]{:S(2)}) async-start(), calls=%async_computation.124 | async-start | bytes 589824
  1489.9 810.7 %reduce-scatter.167.cloned.1.call-start = ((), (), s32[]{:S(2)}) async-start(), calls=%async_computation.123 | async-start | bytes 589824
  1491.5 877.1 %reduce-scatter.145.cloned.1.call-start = ((), (), s32[]{:S(2)}) async-start(), calls=%async_computation.108 | async-start | bytes 1769472 | tf_op jit(solution)/shard_map/reduce_scatter | solution.py:89
  1495.0 941.9 %reduce-scatter.143.cloned.1.call-start = ((), (), s32[]{:S(2)}) async-start(), calls=%async_computation.107 | async-start | bytes 1769472 | tf_op jit(solution)/shard_map/reduce_scatter | solution.py:89
  1498.6 1006.1 %reduce-scatter.141.cloned.1.call-start = ((), (), s32[]{:S(2)}) async-start(), calls=%async_computation.106 | async-start | bytes 1769472 | tf_op jit(solution)/shard_map/reduce_scatter | solution.py:89
  1502.3 1070.8 %reduce-scatter.147.cloned.1.call-start = ((), (), s32[]{:S(2)}) async-start(), calls=%async_computation.109 | async-start | bytes 1769472 | tf_op jit(solution)/shard_map/reduce_scatter | solution.py:89
  1504.6 1132.7 %reduce-scatter.127.cloned.1.call-start = ((), (), s32[]{:S(2)}) async-start(), calls=%async_computation.99 | async-start | bytes 589824 | tf_op jit(solution)/shard_map/reduce_scatter | solution.py:77
  1505.8 1196.0 %reduce-scatter.129.cloned.1.call-start = ((), (), s32[]{:S(2)}) async-start(), calls=%async_computation.100 | async-start | bytes 589824 | tf_op jit(solution)/shard_map/reduce_scatter | solution.py:77
  1507.0 1258.9 %reduce-scatter.125.cloned.1.call-start = ((), (), s32[]{:S(2)}) async-start(), calls=%async_computation.98 | async-start | bytes 589824 | tf_op jit(solution)/shard_map/reduce_scatter | solution.py:77
  1509.3 1321.4 %reduce-scatter.131.cloned.1.call-start = ((), (), s32[]{:S(2)}) async-start(), calls=%async_computation.101 | async-start | bytes 589824 | tf_op jit(solution)/shard_map/reduce_scatter | solution.py:77
  1510.7 1385.8 %reduce-scatter.117.cloned.1.call-start = ((), (), s32[]{:S(2)}) async-start(), calls=%async_computation.91 | async-start | bytes 1179648 | tf_op jit(solution)/shard_map/reduce_scatter | solution.py:71
  1523.7 1438.9 %reduce-scatter.119.cloned.1.call-start = ((), (), s32[]{:S(2)}) async-start(), calls=%async_computation.93 | async-start | bytes 1179648 | tf_op jit(solution)/shard_map/reduce_scatter | solution.py:71
  1537.6 1490.9 %reduce-scatter.121.cloned.1.call-start = ((), (), s32[]{:S(2)}) async-start(), calls=%async_computation.95 | async-start | bytes 1179648 | tf_op jit(solution)/shard_map/reduce_scatter | solution.py:71
  1550.6 1543.8 %reduce-scatter.123.cloned.1.call-start = ((), (), s32[]{:S(2)}) async-start(), calls=%async_computation.97 | async-start | bytes 1179648 | tf_op jit(solution)/shard_map/reduce_scatter | solution.py:71
  1564.9 1596.6 %reduce-scatter.157.cloned.1.call-start = ((), (), s32[]{:S(2)}) async-start(), calls=%async_computation.118 | async-start | bytes 1769472
  1571.3 1657.6 %reduce-scatter.159.cloned.1.call-start = ((), (), s32[]{:S(2)}) async-start(), calls=%async_computation.119 | async-start | bytes 1769472
  1577.7 1718.4 %reduce-scatter.161.cloned.1.call-start = ((), (), s32[]{:S(2)}) async-start(), calls=%async_computation.120 | async-start | bytes 1769472
  1584.1 1779.5 %reduce-scatter.163.cloned.1.call-start = ((), (), s32[]{:S(2)}) async-start(), calls=%async_computation.121 | async-start | bytes 1769472
  1590.6 1843.8 %reduce-scatter.135.cloned.1.call-start = ((), (), s32[]{:S(2)}) async-start(), calls=%async_computation.103 | async-start | bytes 2359296 | tf_op jit(solution)/shard_map/reduce_scatter | solution.py:80
  1593.0 1912.2 %reduce-scatter.137.cloned.1.call-start = ((), (), s32[]{:S(2)}) async-start(), calls=%async_computation.104 | async-start | bytes 2359296 | tf_op jit(solution)/shard_map/reduce_scatter | solution.py:80
  1595.2 1980.9 %reduce-scatter.133.cloned.1.call-start = ((), (), s32[]{:S(2)}) async-start(), calls=%async_computation.102 | async-start | bytes 2359296 | tf_op jit(solution)/shard_map/reduce_scatter | solution.py:80
  1597.4 2049.5 %reduce-scatter.139.cloned.1.call-start = ((), (), s32[]{:S(2)}) async-start(), calls=%async_computation.105 | async-start | bytes 2359296 | tf_op jit(solution)/shard_map/reduce_scatter | solution.py:80
  (250 other events, 20175.1 us)
Sparse Core Ops, SparseCore 0:
  10.1 42.8 all-gather.30
  55.1 44.4 all-gather.32
  110.5 51.0 all-reduce.50
  163.7 51.1 all-gather.34
  218.7 29.6 reduce-scatter.76
  250.7 31.4 reduce-scatter.82
  284.9 31.4 reduce-scatter.88
  318.9 31.4 reduce-scatter.94
  352.8 49.4 all-gather.38
  479.4 31.4 reduce-scatter.96
  513.3 31.4 reduce-scatter.90
  547.3 31.4 reduce-scatter.84
  581.1 31.4 reduce-scatter.78
  614.8 49.2 all-gather.42
  702.3 51.0 all-gather.44
  828.7 16.8 all-gather.40
  866.6 31.4 reduce-scatter.112
  900.6 31.4 reduce-scatter.108
  934.6 31.4 reduce-scatter.104
  968.6 31.4 reduce-scatter.100
  1002.8 31.4 reduce-scatter.98
  1036.6 31.4 reduce-scatter.80
  1070.8 31.4 reduce-scatter.92
  1104.8 31.4 reduce-scatter.86
  1138.3 16.8 all-gather.64
  1213.7 31.4 reduce-scatter.114
  1247.7 31.4 reduce-scatter.102
  1281.9 31.4 reduce-scatter.110
  1315.7 31.4 reduce-scatter.106
  1363.6 17.8 all-gather.68
  1420.3 16.8 all-gather.72
  1442.9 36.5 all-reduce.52
  1482.8 68.3 reduce-scatter.178
  1554.7 66.5 reduce-scatter.176
  1624.7 66.6 reduce-scatter.174
  1694.9 66.6 reduce-scatter.172
  1765.0 66.6 reduce-scatter.154
  1835.2 66.7 reduce-scatter.152
  1905.5 66.6 reduce-scatter.150
  1975.7 66.6 reduce-scatter.148
  2046.3 60.8 reduce-scatter.170
  2110.8 60.9 reduce-scatter.164
  2175.0 60.8 reduce-scatter.168
  2239.6 61.0 reduce-scatter.166
  2304.1 64.4 reduce-scatter.144
  2372.5 64.4 reduce-scatter.142
  2440.3 64.4 reduce-scatter.140
  2508.5 64.5 reduce-scatter.146
  2576.4 60.8 reduce-scatter.126
  2640.8 60.9 reduce-scatter.128
  2705.0 60.9 reduce-scatter.124
  2769.6 60.9 reduce-scatter.130
  2834.1 62.3 reduce-scatter.116
  2900.1 62.4 reduce-scatter.118
  2966.1 62.3 reduce-scatter.120
  3032.1 62.3 reduce-scatter.122
  3097.7 63.7 reduce-scatter.156
  3165.2 63.7 reduce-scatter.158
  3232.4 63.7 reduce-scatter.160
  3299.8 63.7 reduce-scatter.162
  3367.1 67.2 reduce-scatter.134
  3438.0 67.1 reduce-scatter.136
  3508.7 67.3 reduce-scatter.132
  3579.7 67.1 reduce-scatter.138
  (16 shorter events, 263.8 us)
where the time goes:
time: 3670 us; the launch traced here: 3660 us
  waiting for transfers between devices  2990 us (81%)
  matrix products  239 us (7%)
  local copies, waits for them, and re-layouts  152 us (4%)
  blocking collectives  141 us (4%)
  other arithmetic  64.4 us (2%)
  starting transfers between devices  47.6 us (1%)
    unnamed x92, waiting for transfers between devices  686 us
    reduce_scatter x20, waiting for transfers between devices, share_rows(): return lax.psum_scatter(value, 'cond', scatter_dimension=1, tiled=True)  554 us
    reduce_scatter x4, waiting for transfers between devices, spread_grads(): lax.psum_scatter(gradients[3].astype(jnp.bfloat16), 'seq', scatter_dimens...  281 us
    reduce_scatter x4, waiting for transfers between devices, spread_grads(): lax.psum_scatter(gradients[10].astype(jnp.bfloat16), 'seq', scatter_dimen...  278 us
    reduce_scatter x4, waiting for transfers between devices, spread_grads(): lax.psum_scatter(gradients[6].astype(jnp.bfloat16), 'seq', scatter_dimens...  271 us
    reduce_scatter x4, waiting for transfers between devices, spread_grads(): lax.psum_scatter(gradients[0].astype(jnp.bfloat16), 'seq', scatter_dimens...  262 us
    reduce_scatter x4, waiting for transfers between devices, spread_grads(): lax.psum_scatter(gradients[2].astype(jnp.bfloat16), 'seq', scatter_dimens...  232 us
    all_gather x20, waiting for transfers between devices, gather_rows(): return lax.all_gather(value, 'cond', axis=1, tiled=True)  185 us
  transfers between devices with their start and end apart: 96, of which 85 were waited for; matrix products, arithmetic and copies ran while one was open for 11% of the time, Pallas kernels for 0%

commit v1 on v0

--- a/solution.py
+++ b/solution.py
@@ -9,6 +9,24 @@
 CONV_DILATION = 27
 EPSILON = 1e-05
 NEG_FILL = -1e30
+
+
+def gather_around(value, axis, dim):
+    ways, here, step = (lax.axis_size(axis), lax.axis_index(axis), value.shape[dim])
+    lengths = [n * ways if d == dim else n for d, n in enumerate(value.shape)]
+    full = lax.dynamic_update_slice_in_dim(
+        jnp.zeros(lengths, value.dtype), value, here * step, axis=dim
+    )
+    going_up = going_down = value
+    for far in range(1, ways // 2 + 1):
+        going_up = lax.ppermute(going_up, axis, [(d, (d + 1) % ways) for d in range(ways)])
+        full = lax.dynamic_update_slice_in_dim(full, going_up, (here - far) % ways * step, axis=dim)
+        if 2 * far < ways:
+            going_down = lax.ppermute(going_down, axis, [(d, (d - 1) % ways) for d in range(ways)])
+            full = lax.dynamic_update_slice_in_dim(
+                full, going_down, (here + far) % ways * step, axis=dim
+            )
+    return full
 
 
 def extended(cells, sides, width):
@@ -108,7 +126,7 @@
 
 
 def gather_rows(value):
-    return lax.all_gather(value, "cond", axis=1, tiled=True)
+    return gather_around(value, "cond", 1)
 
 
 def share_rows(value):

time: 3670 us -> 3460 us (0.943)
  waiting for transfers between devices: 2990 us -> 2680 us
  starting transfers between devices: 47.6 us -> 106 us
  local copies, waits for them, and re-layouts: 152 us -> 210 us
    reduce_scatter x20, waiting for transfers between devices: 554 us -> 297 us  [share_rows(): return lax.psum_scatter(value, 'cond', scatter_dimension=1, tiled=True)]
    all_gather x20 -> x0, waiting for transfers between devices: 185 us -> none  [gather_rows(): return lax.all_gather(value, 'cond', axis=1, tiled=True)]
    ppermute x0 -> x60, waiting for transfers between devices: none -> 165 us  [the longest x40 146 us: gather_around(): lax.ppermute(going_up, axis, [(d, (d + 1) % ways) for d in range(ways)])]
    ppermute x0 -> x60, starting transfers between devices: none -> 59.6 us  [the longest x40 35.6 us: gather_around(): lax.ppermute(going_up, axis, [(d, (d + 1) % ways) for d in range(ways)])]
    unnamed x485 -> x573, local copies, waits for them, and re-layouts: 76.7 us -> 89.5 us
    unnamed x92 -> x72, waiting for transfers between devices: 686 us -> 675 us
  transfers between devices with their start and end apart: 96 -> 136, of which waited for: 85 -> 91; matrix products, arithmetic and copies ran while one was open for 11% -> 11% of each run, Pallas kernels for 0% -> 0%
where the time goes in v1:
time: 3460 us; the launch traced here: 3450 us
  waiting for transfers between devices  2680 us (77%)
  matrix products  217 us (6%)
  local copies, waits for them, and re-layouts  210 us (6%)
  blocking collectives  143 us (4%)
  starting transfers between devices  106 us (3%)
  other arithmetic  69.5 us (2%)
    unnamed x72, waiting for transfers between devices  675 us
    reduce_scatter x20, waiting for transfers between devices, share_rows(): return lax.psum_scatter(value, 'cond', scatter_dimension=1, tiled=True)  297 us
    reduce_scatter x4, waiting for transfers between devices, spread_grads(): lax.psum_scatter(gradients[3].astype(jnp.bfloat16), 'seq', scatter_dimens...  281 us
    reduce_scatter x4, waiting for transfers between devices, spread_grads(): lax.psum_scatter(gradients[10].astype(jnp.bfloat16), 'seq', scatter_dimen...  277 us
    reduce_scatter x4, waiting for transfers between devices, spread_grads(): lax.psum_scatter(gradients[6].astype(jnp.bfloat16), 'seq', scatter_dimens...  271 us
    reduce_scatter x4, waiting for transfers between devices, spread_grads(): lax.psum_scatter(gradients[0].astype(jnp.bfloat16), 'seq', scatter_dimens...  262 us
    reduce_scatter x4, waiting for transfers between devices, spread_grads(): lax.psum_scatter(gradients[2].astype(jnp.bfloat16), 'seq', scatter_dimens...  232 us
    ppermute x40, waiting for transfers between devices, gather_around(): lax.ppermute(going_up, axis, [(d, (d + 1) % ways) for d in range(ways)])  146 us
  transfers between devices with their start and end apart: 136, of which 91 were waited for; matrix products, arithmetic and copies ran while one was open for 11% of the time, Pallas kernels for 0%

profile of v1, /device:TPU:0, one launch (start us, length us, event | category | flops | bytes accessed | tf_op | source)
XLA Modules:
  0.0 3448.0 jit_solution(5862453600844652258)
XLA Ops:
  9.6 43.5 %all-gather.7.cloned.1.call-done = bf16[2048,256]{1,0:T(8,128)(2,1)} async-done(((bf16[256,256]{1,0:T(8,128)(2,1)}), bf16[2048,256]{1,0:T(8,128)(2,1)}) %all-gather.7.cloned.1.call-update) | async-done | bytes 1048592 | tf_op jit(solution)/shard_map/all_gather | solution.py:72
  78.9 20.4 all-gather.9.cloned.1.call-done
  109.5 31.4 all_gather.26
  140.9 19.0 all-reduce.51.cloned.1.call-done
  164.6 48.5 %all-gather.11.cloned.1.call-done = bf16[256,4096]{1,0:T(8,128)(2,1)} async-done(((bf16[256,512]{1,0:T(8,128)(2,1)}), bf16[256,4096]{1,0:T(8,128)(2,1)}) %all-gather.11.cloned.1.call-update) | async-done | bytes 2097168 | tf_op jit(solution)/shard_map/all_gather | solution.py:75
  244.2 19.8 all-reduce.46
  264.1 16.4 reduce-scatter.95.cloned.1.call-done
  280.5 34.2 reduce-scatter.83.cloned.1.call-done
  314.7 34.0 reduce-scatter.77.cloned.1.call-done
  351.1 10.7 all-reduce.43
  370.0 31.1 all_gather.31
  479.2 9.3 collective-permute-done.26
  514.2 12.0 collective-permute-done.38
  531.7 32.5 reduce-scatter.97.cloned.1.call-done
  565.5 10.1 all-reduce.42
  592.7 23.1 all-gather.15.cloned.1.call-done
  620.3 47.2 %all-gather.17.cloned.1.call-done = bf16[1024,1024]{1,0:T(8,128)(2,1)} async-done(((bf16[1024,128]{1,0:T(8,128)(2,1)}), bf16[1024,1024]{1,0:T(8,128)(2,1)}) %all-gather.17.cloned.1.call-update) | async-done | bytes 2097168 | tf_op jit(solution)/shard_map/all_gather | solution.py:83
  667.5 8.8 add_convert_fusion.2
  693.6 10.4 collective-permute-done.21
  704.2 11.2 collective-permute-done.23
  718.1 6.8 add_convert_fusion.1
  738.1 10.2 collective-permute-done.51
  748.3 9.7 collective-permute-done.29
  766.8 6.8 add_convert_fusion
  795.6 9.2 collective-permute-done.5
  835.4 34.0 reduce-scatter.99.cloned.1.call-done
  869.4 34.0 reduce-scatter.113.cloned.1.call-done
  903.4 34.2 reduce-scatter.81.cloned.1.call-done
  937.5 34.0 reduce-scatter.101.cloned.1.call-done
  975.4 10.3 all-reduce.41
  1135.1 33.9 reduce-scatter.103.cloned.1.call-done
  1172.3 10.1 all-reduce.40
  1399.2 14.6 reduce-scatter.177.cloned.1.call-done
  1414.9 69.3 %reduce-scatter.179.cloned.1.call-done = bf16[128,1024]{1,0:T(8,128)(2,1)} async-done(((bf16[1024,1024]{1,0:T(8,128)(2,1)}), bf16[128,1024]{1,0:T(8,128)(2,1)}) %reduce-scatter.179.cloned.1.call-update) | async-done | bytes 262160
  1485.4 69.5 %reduce-scatter.173.cloned.1.call-done = bf16[128,1024]{1,0:T(8,128)(2,1)} async-done(((bf16[1024,1024]{1,0:T(8,128)(2,1)}), bf16[128,1024]{1,0:T(8,128)(2,1)}) %reduce-scatter.173.cloned.1.call-update) | async-done | bytes 262160
  1558.2 66.8 %reduce-scatter.151.cloned.1.call-done = bf16[128,1024]{1,0:T(8,128)(2,1)} async-done(((bf16[1024,1024]{1,0:T(8,128)(2,1)}), bf16[128,1024]{1,0:T(8,128)(2,1)}) %reduce-scatter.151.cloned.1.call-update) | async-done | bytes 262160 | tf_op jit(solution)/shard_map/reduce_scatter | solution.py:119
  1625.0 70.1 %reduce-scatter.153.cloned.1.call-done = bf16[128,1024]{1,0:T(8,128)(2,1)} async-done(((bf16[1024,1024]{1,0:T(8,128)(2,1)}), bf16[128,1024]{1,0:T(8,128)(2,1)}) %reduce-scatter.153.cloned.1.call-update) | async-done | bytes 262160 | tf_op jit(solution)/shard_map/reduce_scatter | solution.py:119
  1695.2 70.3 %reduce-scatter.155.cloned.1.call-done = bf16[128,1024]{1,0:T(8,128)(2,1)} async-done(((bf16[1024,1024]{1,0:T(8,128)(2,1)}), bf16[128,1024]{1,0:T(8,128)(2,1)}) %reduce-scatter.155.cloned.1.call-update) | async-done | bytes 262160 | tf_op jit(solution)/shard_map/reduce_scatter | solution.py:119
  1765.5 70.0 %reduce-scatter.149.cloned.1.call-done = bf16[128,1024]{1,0:T(8,128)(2,1)} async-done(((bf16[1024,1024]{1,0:T(8,128)(2,1)}), bf16[128,1024]{1,0:T(8,128)(2,1)}) %reduce-scatter.149.cloned.1.call-update) | async-done | bytes 262160 | tf_op jit(solution)/shard_map/reduce_scatter | solution.py:119
  1837.6 62.0 %reduce-scatter.167.cloned.1.call-done = bf16[128,256]{1,0:T(8,128)(2,1)} async-done(((bf16[1024,256]{1,0:T(8,128)(2,1)}), bf16[128,256]{1,0:T(8,128)(2,1)}) %reduce-scatter.167.cloned.1.call-update) | async-done | bytes 65552
  1900.6 63.7 %reduce-scatter.169.cloned.1.call-done = bf16[128,256]{1,0:T(8,128)(2,1)} async-done(((bf16[1024,256]{1,0:T(8,128)(2,1)}), bf16[128,256]{1,0:T(8,128)(2,1)}) %reduce-scatter.169.cloned.1.call-update) | async-done | bytes 65552
  1965.3 63.1 %reduce-scatter.165.cloned.1.call-done = bf16[128,256]{1,0:T(8,128)(2,1)} async-done(((bf16[1024,256]{1,0:T(8,128)(2,1)}), bf16[128,256]{1,0:T(8,128)(2,1)}) %reduce-scatter.165.cloned.1.call-update) | async-done | bytes 65552
  2029.3 63.9 %reduce-scatter.171.cloned.1.call-done = bf16[128,256]{1,0:T(8,128)(2,1)} async-done(((bf16[1024,256]{1,0:T(8,128)(2,1)}), bf16[128,256]{1,0:T(8,128)(2,1)}) %reduce-scatter.171.cloned.1.call-update) | async-done | bytes 65552
  2094.8 66.4 %reduce-scatter.143.cloned.1.call-done = bf16[128,3,256]{2,0,1:T(8,128)(2,1)} async-done(((bf16[1024,3,256]{2,0,1:T(8,128)(2,1)}), bf16[128,3,256]{2,0,1:T(8,128)(2,1)}) %reduce-scatter.143.cloned.1.call-update) | async-done | bytes 196624 | tf_op jit(solution)/shard_map/reduce_scatter | solution.py:107
  2161.2 68.3 %reduce-scatter.145.cloned.1.call-done = bf16[128,3,256]{2,0,1:T(8,128)(2,1)} async-done(((bf16[1024,3,256]{2,0,1:T(8,128)(2,1)}), bf16[128,3,256]{2,0,1:T(8,128)(2,1)}) %reduce-scatter.145.cloned.1.call-update) | async-done | bytes 196624 | tf_op jit(solution)/shard_map/reduce_scatter | solution.py:107
  2229.5 67.8 %reduce-scatter.141.cloned.1.call-done = bf16[128,3,256]{2,0,1:T(8,128)(2,1)} async-done(((bf16[1024,3,256]{2,0,1:T(8,128)(2,1)}), bf16[128,3,256]{2,0,1:T(8,128)(2,1)}) %reduce-scatter.141.cloned.1.call-update) | async-done | bytes 196624 | tf_op jit(solution)/shard_map/reduce_scatter | solution.py:107
  2297.3 68.2 %reduce-scatter.147.cloned.1.call-done = bf16[128,3,256]{2,0,1:T(8,128)(2,1)} async-done(((bf16[1024,3,256]{2,0,1:T(8,128)(2,1)}), bf16[128,3,256]{2,0,1:T(8,128)(2,1)}) %reduce-scatter.147.cloned.1.call-update) | async-done | bytes 196624 | tf_op jit(solution)/shard_map/reduce_scatter | solution.py:107
  2367.6 19.8 all-reduce.45
  2390.9 38.6 %reduce-scatter.125.cloned.1.call-done = bf16[128,256]{1,0:T(8,128)(2,1)} async-done(((bf16[1024,256]{1,0:T(8,128)(2,1)}), bf16[128,256]{1,0:T(8,128)(2,1)}) %reduce-scatter.125.cloned.1.call-update) | async-done | bytes 65552 | tf_op jit(solution)/shard_map/reduce_scatter | solution.py:95
  2429.6 64.4 %reduce-scatter.127.cloned.1.call-done = bf16[128,256]{1,0:T(8,128)(2,1)} async-done(((bf16[1024,256]{1,0:T(8,128)(2,1)}), bf16[128,256]{1,0:T(8,128)(2,1)}) %reduce-scatter.127.cloned.1.call-update) | async-done | bytes 65552 | tf_op jit(solution)/shard_map/reduce_scatter | solution.py:95
  2494.0 64.2 %reduce-scatter.129.cloned.1.call-done = bf16[128,256]{1,0:T(8,128)(2,1)} async-done(((bf16[1024,256]{1,0:T(8,128)(2,1)}), bf16[128,256]{1,0:T(8,128)(2,1)}) %reduce-scatter.129.cloned.1.call-update) | async-done | bytes 65552 | tf_op jit(solution)/shard_map/reduce_scatter | solution.py:95
  2558.2 64.6 %reduce-scatter.131.cloned.1.call-done = bf16[128,256]{1,0:T(8,128)(2,1)} async-done(((bf16[1024,256]{1,0:T(8,128)(2,1)}), bf16[128,256]{1,0:T(8,128)(2,1)}) %reduce-scatter.131.cloned.1.call-update) | async-done | bytes 65552 | tf_op jit(solution)/shard_map/reduce_scatter | solution.py:95
  2624.4 64.0 %reduce-scatter.117.cloned.1.call-done = bf16[256,256]{1,0:T(8,128)(2,1)} async-done(((bf16[2048,256]{1,0:T(8,128)(2,1)}), bf16[256,256]{1,0:T(8,128)(2,1)}) %reduce-scatter.117.cloned.1.call-update) | async-done | bytes 131088 | tf_op jit(solution)/shard_map/reduce_scatter | solution.py:89
  2688.3 66.3 %reduce-scatter.119.cloned.1.call-done = bf16[256,256]{1,0:T(8,128)(2,1)} async-done(((bf16[2048,256]{1,0:T(8,128)(2,1)}), bf16[256,256]{1,0:T(8,128)(2,1)}) %reduce-scatter.119.cloned.1.call-update) | async-done | bytes 131088 | tf_op jit(solution)/shard_map/reduce_scatter | solution.py:89
  2754.6 65.8 %reduce-scatter.121.cloned.1.call-done = bf16[256,256]{1,0:T(8,128)(2,1)} async-done(((bf16[2048,256]{1,0:T(8,128)(2,1)}), bf16[256,256]{1,0:T(8,128)(2,1)}) %reduce-scatter.121.cloned.1.call-update) | async-done | bytes 131088 | tf_op jit(solution)/shard_map/reduce_scatter | solution.py:89
  2820.4 66.3 %reduce-scatter.123.cloned.1.call-done = bf16[256,256]{1,0:T(8,128)(2,1)} async-done(((bf16[2048,256]{1,0:T(8,128)(2,1)}), bf16[256,256]{1,0:T(8,128)(2,1)}) %reduce-scatter.123.cloned.1.call-update) | async-done | bytes 131088 | tf_op jit(solution)/shard_map/reduce_scatter | solution.py:89
  2888.5 65.3 %reduce-scatter.157.cloned.1.call-done = bf16[128,768]{1,0:T(8,128)(2,1)} async-done(((bf16[1024,768]{1,0:T(8,128)(2,1)}), bf16[128,768]{1,0:T(8,128)(2,1)}) %reduce-scatter.157.cloned.1.call-update) | async-done | bytes 196624
  2955.0 66.3 %reduce-scatter.159.cloned.1.call-done = bf16[128,768]{1,0:T(8,128)(2,1)} async-done(((bf16[1024,768]{1,0:T(8,128)(2,1)}), bf16[128,768]{1,0:T(8,128)(2,1)}) %reduce-scatter.159.cloned.1.call-update) | async-done | bytes 196624
  3022.5 66.0 %reduce-scatter.161.cloned.1.call-done = bf16[128,768]{1,0:T(8,128)(2,1)} async-done(((bf16[1024,768]{1,0:T(8,128)(2,1)}), bf16[128,768]{1,0:T(8,128)(2,1)}) %reduce-scatter.161.cloned.1.call-update) | async-done | bytes 196624
  3089.7 66.4 %reduce-scatter.163.cloned.1.call-done = bf16[128,768]{1,0:T(8,128)(2,1)} async-done(((bf16[1024,768]{1,0:T(8,128)(2,1)}), bf16[128,768]{1,0:T(8,128)(2,1)}) %reduce-scatter.163.cloned.1.call-update) | async-done | bytes 196624
  3158.2 68.7 %reduce-scatter.133.cloned.1.call-done = bf16[256,512]{1,0:T(8,128)(2,1)} async-done(((bf16[256,4096]{1,0:T(8,128)(2,1)}), bf16[256,512]{1,0:T(8,128)(2,1)}) %reduce-scatter.133.cloned.1.call-update) | async-done | bytes 262160 | tf_op jit(solution)/shard_map/reduce_scatter | solution.py:98
  3226.9 70.5 %reduce-scatter.135.cloned.1.call-done = bf16[256,512]{1,0:T(8,128)(2,1)} async-done(((bf16[256,4096]{1,0:T(8,128)(2,1)}), bf16[256,512]{1,0:T(8,128)(2,1)}) %reduce-scatter.135.cloned.1.call-update) | async-done | bytes 262160 | tf_op jit(solution)/shard_map/reduce_scatter | solution.py:98
  3297.3 70.7 %reduce-scatter.137.cloned.1.call-done = bf16[256,512]{1,0:T(8,128)(2,1)} async-done(((bf16[256,4096]{1,0:T(8,128)(2,1)}), bf16[256,512]{1,0:T(8,128)(2,1)}) %reduce-scatter.137.cloned.1.call-update) | async-done | bytes 262160 | tf_op jit(solution)/shard_map/reduce_scatter | solution.py:98
  3368.0 70.8 %reduce-scatter.139.cloned.1.call-done = bf16[256,512]{1,0:T(8,128)(2,1)} async-done(((bf16[256,4096]{1,0:T(8,128)(2,1)}), bf16[256,512]{1,0:T(8,128)(2,1)}) %reduce-scatter.139.cloned.1.call-update) | async-done | bytes 262160 | tf_op jit(solution)/shard_map/reduce_scatter | solution.py:98
  (1234 shorter events, 707.8 us)
Async XLA Ops:
  7.2 45.8 %all-gather.7.cloned.1.call-start = ((), (), s32[]{:S(2)}) async-start(), calls=%async_computation.52 | async-start | bytes 1179648 | tf_op jit(solution)/shard_map/all_gather | solution.py:72
  7.9 91.4 %all-gather.9.cloned.1.call-start = ((), (), s32[]{:S(2)}) async-start(), calls=%async_computation.53 | async-start | bytes 1769472 | tf_op jit(solution)/shard_map/all_gather | solution.py:73
  8.7 151.2 %all-reduce.51.cloned.1.call-start = ((), (), s32[]{:S(2)}) async-start(), calls=%async_computation.110 | async-start | bytes 4194304 | tf_op jit(solution)/shard_map/psum | solution.py:199
  60.0 42.0 %collective-permute-start.8 = (bf16[27,256]{1,0:T(8,128)(2,1)S(1)}, bf16[27,256]{1,0:T(8,128)(2,1)S(1)}, u32[]{:S(2)}, u32[]{:S(2)}) collective-permute-start(bf16[27,256]{1,0:T(8,128)(2,1)S(1)} %get-tuple-element.253), channel_id=1, source_target_pairs={{0,1},{1,2},{2,3},{3,4},{4,5},{5,6},{6,7},{8,9},{9,10},{10,11},{11... | collective-permute-start | bytes 41480 | tf_op jit(solution)/shard_map/ppermute | solution.py:40
  64.6 38.7 %collective-permute-start.9 = (bf16[27,256]{1,0:T(8,128)(2,1)S(1)}, bf16[27,256]{1,0:T(8,128)(2,1)S(1)}, u32[]{:S(2)}, u32[]{:S(2)}) collective-permute-start(bf16[27,256]{1,0:T(8,128)(2,1)S(1)} %get-tuple-element.254), channel_id=1, source_target_pairs={{1,0},{2,1},{3,2},{4,3},{5,4},{6,5},{7,6},{9,8},{10,9},{11,10},{12... | collective-permute-start | bytes 41480 | tf_op jit(solution)/shard_map/ppermute | solution.py:42
  108.9 104.3 %all-gather.11.cloned.1.call-start = ((), (), s32[]{:S(2)}) async-start(), calls=%async_computation.54 | async-start | bytes 2359296 | tf_op jit(solution)/shard_map/all_gather | solution.py:75
  109.4 154.6 %reduce-scatter.89.cloned.1.call-start = ((), (), s32[]{:S(2)}) async-start(), calls=%async_computation.64 | async-start | bytes 2621440 | tf_op jit(solution)/shard_map/reduce_scatter | solution.py:133
  216.9 63.6 %reduce-scatter.95.cloned.1.call-start = ((), (), s32[]{:S(2)}) async-start(), calls=%async_computation.67 | async-start | bytes 2621440 | tf_op jit(solution)/shard_map/reduce_scatter | solution.py:133
  223.2 91.4 %reduce-scatter.83.cloned.1.call-start = ((), (), s32[]{:S(2)}) async-start(), calls=%async_computation.61 | async-start | bytes 2621440 | tf_op jit(solution)/shard_map/reduce_scatter | solution.py:133
  234.7 113.9 %reduce-scatter.77.cloned.1.call-start = ((), (), s32[]{:S(2)}) async-start(), calls=%async_computation.55 | async-start | bytes 2621440 | tf_op jit(solution)/shard_map/reduce_scatter | solution.py:133
  241.2 162.1 %all-gather.13.cloned.1.call-start = ((), (), s32[]{:S(2)}) async-start(), calls=%async_computation.56 | async-start | bytes 1769472 | tf_op jit(solution)/shard_map/all_gather | solution.py:78
  241.9 284.3 %reduce-scatter.79.cloned.1.call-start = ((), (), s32[]{:S(2)}) async-start(), calls=%async_computation.57 | async-start | bytes 2621440 | tf_op jit(solution)/shard_map/reduce_scatter | solution.py:133
  420.1 107.4 %reduce-scatter.85.cloned.1.call-start = ((), (), s32[]{:S(2)}) async-start(), calls=%async_computation.62 | async-start | bytes 2621440 | tf_op jit(solution)/shard_map/reduce_scatter | solution.py:133
  447.5 82.3 %reduce-scatter.91.cloned.1.call-start = ((), (), s32[]{:S(2)}) async-start(), calls=%async_computation.65 | async-start | bytes 2621440 | tf_op jit(solution)/shard_map/reduce_scatter | solution.py:133
  477.0 87.3 %reduce-scatter.97.cloned.1.call-start = ((), (), s32[]{:S(2)}) async-start(), calls=%async_computation.68 | async-start | bytes 2621440 | tf_op jit(solution)/shard_map/reduce_scatter | solution.py:133
  509.1 106.7 %all-gather.15.cloned.1.call-start = ((), (), s32[]{:S(2)}) async-start(), calls=%async_computation.58 | async-start | bytes 2359296 | tf_op jit(solution)/shard_map/all_gather | solution.py:82
  509.6 157.8 %all-gather.17.cloned.1.call-start = ((), (), s32[]{:S(2)}) async-start(), calls=%async_computation.59 | async-start | bytes 2359296 | tf_op jit(solution)/shard_map/all_gather | solution.py:83
  510.2 318.7 %reduce-scatter.87.cloned.1.call-start = ((), (), s32[]{:S(2)}) async-start(), calls=%async_computation.63 | async-start | bytes 2621440 | tf_op jit(solution)/shard_map/reduce_scatter | solution.py:133
  512.4 70.7 %collective-permute-start.39 = (bf16[512,256]{1,0:T(8,128)(2,1)}, bf16[512,256]{1,0:T(8,128)(2,1)}, u32[]{:S(2)}, u32[]{:S(2)}) collective-permute-start(bf16[512,256]{1,0:T(8,128)(2,1)} %get-tuple-element.195), channel_id=1, source_target_pairs={{0,24},{8,0},{16,8},{24,16},{1,25},{9,1},{17,9},{25,17},{2,26},{10... | collective-permute-start | bytes 786440 | tf_op jit(solution)/shard_map/ppermute | solution.py:25
  526.2 59.1 %collective-permute-start.40 = (bf16[512,256]{1,0:T(8,128)(2,1)S(1)}, bf16[512,256]{1,0:T(8,128)(2,1)}, u32[]{:S(2)}, u32[]{:S(2)}) collective-permute-start(bf16[512,256]{1,0:T(8,128)(2,1)S(1)} %collective-permute-done.38), channel_id=1, source_target_pairs={{0,8},{8,16},{16,24},{24,0},{1,9},{9,17},{17,25},{25,1},{2,10},{10... | collective-permute-start | bytes 786440 | tf_op jit(solution)/shard_map/ppermute | solution.py:22
  680.7 148.3 %reduce-scatter.105.cloned.1.call-start = ((), (), s32[]{:S(2)}) async-start(), calls=%async_computation.72 | async-start | bytes 2621440 | tf_op jit(solution)/shard_map/reduce_scatter | solution.py:133
  685.4 145.9 %reduce-scatter.93.cloned.1.call-start = ((), (), s32[]{:S(2)}) async-start(), calls=%async_computation.66 | async-start | bytes 2621440 | tf_op jit(solution)/shard_map/reduce_scatter | solution.py:133
  729.0 106.3 %reduce-scatter.109.cloned.1.call-start = ((), (), s32[]{:S(2)}) async-start(), calls=%async_computation.74 | async-start | bytes 2621440 | tf_op jit(solution)/shard_map/reduce_scatter | solution.py:133
  733.9 135.5 %reduce-scatter.99.cloned.1.call-start = ((), (), s32[]{:S(2)}) async-start(), calls=%async_computation.69 | async-start | bytes 2621440 | tf_op jit(solution)/shard_map/reduce_scatter | solution.py:133
  777.7 125.7 %reduce-scatter.113.cloned.1.call-start = ((), (), s32[]{:S(2)}) async-start(), calls=%async_computation.76 | async-start | bytes 2621440 | tf_op jit(solution)/shard_map/reduce_scatter | solution.py:133
  782.4 155.2 %reduce-scatter.81.cloned.1.call-start = ((), (), s32[]{:S(2)}) async-start(), calls=%async_computation.60 | async-start | bytes 2621440 | tf_op jit(solution)/shard_map/reduce_scatter | solution.py:133
  824.3 147.3 %reduce-scatter.101.cloned.1.call-start = ((), (), s32[]{:S(2)}) async-start(), calls=%async_computation.70 | async-start | bytes 2621440 | tf_op jit(solution)/shard_map/reduce_scatter | solution.py:133
  828.9 300.9 %reduce-scatter.107.cloned.1.call-start = ((), (), s32[]{:S(2)}) async-start(), calls=%async_computation.73 | async-start | bytes 2621440 | tf_op jit(solution)/shard_map/reduce_scatter | solution.py:133
  1023.4 106.4 %reduce-scatter.111.cloned.1.call-start = ((), (), s32[]{:S(2)}) async-start(), calls=%async_computation.75 | async-start | bytes 2621440 | tf_op jit(solution)/shard_map/reduce_scatter | solution.py:133
  1060.7 74.3 %reduce-scatter.115.cloned.1.call-start = ((), (), s32[]{:S(2)}) async-start(), calls=%async_computation.77 | async-start | bytes 2621440 | tf_op jit(solution)/shard_map/reduce_scatter | solution.py:133
  1100.0 69.0 %reduce-scatter.103.cloned.1.call-start = ((), (), s32[]{:S(2)}) async-start(), calls=%async_computation.71 | async-start | bytes 2621440 | tf_op jit(solution)/shard_map/reduce_scatter | solution.py:133
  1129.7 178.0 %all-reduce.53.cloned.1.call-start = ((), (), s32[]{:S(2)}) async-start(), calls=%async_computation.111 | async-start | bytes 2097152 | tf_op jit(solution)/shard_map/psum | solution.py:305
  1234.4 163.7 %reduce-scatter.175.cloned.1.call-start = ((), (), s32[]{:S(2)}) async-start(), calls=%async_computation.107 | async-start | bytes 2359296
  1239.9 173.9 %reduce-scatter.177.cloned.1.call-start = ((), (), s32[]{:S(2)}) async-start(), calls=%async_computation.108 | async-start | bytes 2359296
  1245.5 238.7 %reduce-scatter.179.cloned.1.call-start = ((), (), s32[]{:S(2)}) async-start(), calls=%async_computation.109 | async-start | bytes 2359296
  1251.2 303.7 %reduce-scatter.173.cloned.1.call-start = ((), (), s32[]{:S(2)}) async-start(), calls=%async_computation.106 | async-start | bytes 2359296
  1256.7 368.3 %reduce-scatter.151.cloned.1.call-start = ((), (), s32[]{:S(2)}) async-start(), calls=%async_computation.95 | async-start | bytes 2359296 | tf_op jit(solution)/shard_map/reduce_scatter | solution.py:119
  1261.8 433.4 %reduce-scatter.153.cloned.1.call-start = ((), (), s32[]{:S(2)}) async-start(), calls=%async_computation.96 | async-start | bytes 2359296 | tf_op jit(solution)/shard_map/reduce_scatter | solution.py:119
  1266.0 499.5 %reduce-scatter.155.cloned.1.call-start = ((), (), s32[]{:S(2)}) async-start(), calls=%async_computation.97 | async-start | bytes 2359296 | tf_op jit(solution)/shard_map/reduce_scatter | solution.py:119
  1270.1 565.4 %reduce-scatter.149.cloned.1.call-start = ((), (), s32[]{:S(2)}) async-start(), calls=%async_computation.94 | async-start | bytes 2359296 | tf_op jit(solution)/shard_map/reduce_scatter | solution.py:119
  1274.3 625.3 %reduce-scatter.167.cloned.1.call-start = ((), (), s32[]{:S(2)}) async-start(), calls=%async_computation.103 | async-start | bytes 589824
  1278.8 685.5 %reduce-scatter.169.cloned.1.call-start = ((), (), s32[]{:S(2)}) async-start(), calls=%async_computation.104 | async-start | bytes 589824
  1283.2 745.1 %reduce-scatter.165.cloned.1.call-start = ((), (), s32[]{:S(2)}) async-start(), calls=%async_computation.102 | async-start | bytes 589824
  1286.6 806.6 %reduce-scatter.171.cloned.1.call-start = ((), (), s32[]{:S(2)}) async-start(), calls=%async_computation.105 | async-start | bytes 589824
  1289.1 872.1 %reduce-scatter.143.cloned.1.call-start = ((), (), s32[]{:S(2)}) async-start(), calls=%async_computation.91 | async-start | bytes 1769472 | tf_op jit(solution)/shard_map/reduce_scatter | solution.py:107
  1293.1 936.4 %reduce-scatter.145.cloned.1.call-start = ((), (), s32[]{:S(2)}) async-start(), calls=%async_computation.92 | async-start | bytes 1769472 | tf_op jit(solution)/shard_map/reduce_scatter | solution.py:107
  1295.3 1001.9 %reduce-scatter.141.cloned.1.call-start = ((), (), s32[]{:S(2)}) async-start(), calls=%async_computation.90 | async-start | bytes 1769472 | tf_op jit(solution)/shard_map/reduce_scatter | solution.py:107
  1299.2 1066.3 %reduce-scatter.147.cloned.1.call-start = ((), (), s32[]{:S(2)}) async-start(), calls=%async_computation.93 | async-start | bytes 1769472 | tf_op jit(solution)/shard_map/reduce_scatter | solution.py:107
  1302.6 1126.9 %reduce-scatter.125.cloned.1.call-start = ((), (), s32[]{:S(2)}) async-start(), calls=%async_computation.82 | async-start | bytes 589824 | tf_op jit(solution)/shard_map/reduce_scatter | solution.py:95
  1303.9 1190.1 %reduce-scatter.127.cloned.1.call-start = ((), (), s32[]{:S(2)}) async-start(), calls=%async_computation.83 | async-start | bytes 589824 | tf_op jit(solution)/shard_map/reduce_scatter | solution.py:95
  1305.1 1253.1 %reduce-scatter.129.cloned.1.call-start = ((), (), s32[]{:S(2)}) async-start(), calls=%async_computation.84 | async-start | bytes 589824 | tf_op jit(solution)/shard_map/reduce_scatter | solution.py:95
  1306.3 1316.4 %reduce-scatter.131.cloned.1.call-start = ((), (), s32[]{:S(2)}) async-start(), calls=%async_computation.85 | async-start | bytes 589824 | tf_op jit(solution)/shard_map/reduce_scatter | solution.py:95
  1307.7 1380.7 %reduce-scatter.117.cloned.1.call-start = ((), (), s32[]{:S(2)}) async-start(), calls=%async_computation.78 | async-start | bytes 1179648 | tf_op jit(solution)/shard_map/reduce_scatter | solution.py:89
  1320.9 1433.7 %reduce-scatter.119.cloned.1.call-start = ((), (), s32[]{:S(2)}) async-start(), calls=%async_computation.79 | async-start | bytes 1179648 | tf_op jit(solution)/shard_map/reduce_scatter | solution.py:89
  1335.4 1485.0 %reduce-scatter.121.cloned.1.call-start = ((), (), s32[]{:S(2)}) async-start(), calls=%async_computation.80 | async-start | bytes 1179648 | tf_op jit(solution)/shard_map/reduce_scatter | solution.py:89
  1348.9 1537.7 %reduce-scatter.123.cloned.1.call-start = ((), (), s32[]{:S(2)}) async-start(), calls=%async_computation.81 | async-start | bytes 1179648 | tf_op jit(solution)/shard_map/reduce_scatter | solution.py:89
  1362.8 1591.0 %reduce-scatter.157.cloned.1.call-start = ((), (), s32[]{:S(2)}) async-start(), calls=%async_computation.98 | async-start | bytes 1769472
  1369.1 1652.2 %reduce-scatter.159.cloned.1.call-start = ((), (), s32[]{:S(2)}) async-start(), calls=%async_computation.99 | async-start | bytes 1769472
  1375.5 1713.0 %reduce-scatter.161.cloned.1.call-start = ((), (), s32[]{:S(2)}) async-start(), calls=%async_computation.100 | async-start | bytes 1769472
  1381.9 1774.2 %reduce-scatter.163.cloned.1.call-start = ((), (), s32[]{:S(2)}) async-start(), calls=%async_computation.101 | async-start | bytes 1769472
  1388.4 1838.4 %reduce-scatter.133.cloned.1.call-start = ((), (), s32[]{:S(2)}) async-start(), calls=%async_computation.86 | async-start | bytes 2359296 | tf_op jit(solution)/shard_map/reduce_scatter | solution.py:98
  1390.8 1906.5 %reduce-scatter.135.cloned.1.call-start = ((), (), s32[]{:S(2)}) async-start(), calls=%async_computation.87 | async-start | bytes 2359296 | tf_op jit(solution)/shard_map/reduce_scatter | solution.py:98
  1393.0 1975.0 %reduce-scatter.137.cloned.1.call-start = ((), (), s32[]{:S(2)}) async-start(), calls=%async_computation.88 | async-start | bytes 2359296 | tf_op jit(solution)/shard_map/reduce_scatter | solution.py:98
  1395.2 2043.7 %reduce-scatter.139.cloned.1.call-start = ((), (), s32[]{:S(2)}) async-start(), calls=%async_computation.89 | async-start | bytes 2359296 | tf_op jit(solution)/shard_map/reduce_scatter | solution.py:98
  (334 other events, 18399.4 us)
Sparse Core Ops, SparseCore 0:
  10.1 42.8 all-gather.6
  55.1 44.1 all-gather.8
  109.0 50.8 all-reduce.50
  162.0 51.1 all-gather.10
  217.0 29.6 reduce-scatter.88
  249.0 31.4 reduce-scatter.94
  283.2 31.4 reduce-scatter.82
  317.2 31.4 reduce-scatter.76
  351.1 48.7 all-gather.12
  420.2 30.7 reduce-scatter.78
  453.5 34.4 reduce-scatter.84
  490.6 39.2 reduce-scatter.90
  532.4 31.8 reduce-scatter.96
  566.5 49.2 all-gather.14
  617.9 49.5 all-gather.16
  680.8 35.7 reduce-scatter.86
  719.0 37.5 reduce-scatter.104
  759.1 40.0 reduce-scatter.92
  801.7 33.6 reduce-scatter.108
  837.9 31.4 reduce-scatter.98
  871.9 31.4 reduce-scatter.112
  906.1 31.4 reduce-scatter.80
  940.1 31.4 reduce-scatter.100
  1023.5 33.6 reduce-scatter.106
  1060.8 35.8 reduce-scatter.110
  1100.1 34.9 reduce-scatter.114
  1137.4 31.4 reduce-scatter.102
  1234.5 37.6 all-reduce.52
  1275.7 68.1 reduce-scatter.174
  1347.3 66.5 reduce-scatter.176
  1417.4 66.8 reduce-scatter.178
  1487.8 67.0 reduce-scatter.172
  1558.3 66.7 reduce-scatter.150
  1628.6 66.5 reduce-scatter.152
  1698.7 66.7 reduce-scatter.154
  1768.9 66.5 reduce-scatter.148
  1838.7 60.9 reduce-scatter.166
  1903.3 60.9 reduce-scatter.168
  1967.5 60.8 reduce-scatter.164
  2032.1 61.0 reduce-scatter.170
  2096.6 64.5 reduce-scatter.142
  2165.1 64.3 reduce-scatter.144
  2232.8 64.4 reduce-scatter.140
  2301.1 64.3 reduce-scatter.146
  2368.7 60.8 reduce-scatter.124
  2433.1 60.8 reduce-scatter.126
  2497.2 60.9 reduce-scatter.128
  2561.8 60.9 reduce-scatter.130
  2626.0 62.2 reduce-scatter.116
  2692.1 62.4 reduce-scatter.118
  2757.9 62.4 reduce-scatter.120
  2824.2 62.4 reduce-scatter.122
  2889.9 63.8 reduce-scatter.156
  2957.6 63.6 reduce-scatter.158
  3024.7 63.7 reduce-scatter.160
  3092.3 63.7 reduce-scatter.162
  3159.6 67.1 reduce-scatter.132
  3230.2 67.0 reduce-scatter.134
  3300.7 67.2 reduce-scatter.136
  3371.6 67.2 reduce-scatter.138
